TPU v7x, 128 devices: a whole 4x4x4 slice. The times are simulated.
128 devices in a mesh: det: 16 (over z, y_hi, core), band: 8 (over y_lo, x).
Axes of the slice: x: 4, y: 4 (y_hi: 2, y_lo: 2; y = y_hi * 2 + y_lo), z: 4, core: 2. Of those that a mesh axis runs over, the one named last changes fastest.
Arguments:
- scan_lines: float32 [1024, 4096], P(('det', 'band')), may hold values from -6 to 6
- response: float32 [1024, 4096], P(('det', 'band')), may hold values from 0.02 to 1
- cycle_offset: int32 [1024, 4096], P(('det', 'band')), may hold values from 0 to 127
- column: int32 [1024, 4096], P(('det', 'band')), may hold values from 0 to 2047
- order_slot: int32 [256], replicated, may hold values from 0 to 255, each once
- legendre: float32 [256, 1024, 1024], P('det', 'band'), may hold values from -0.046875 to 0.046875
Outputs:
- harmonics: float32 [2, 256, 1024], P(None, 'det', 'band')
- sky_map: float32 [1024, 2048], P(('band', 'det'))
Inputs may be any that keep to these rules, and one draw needn't show every extreme that they name: `order_slot`: each of the orders 0 to 255 stands in exactly one slot.
All inputs are finite; a program needn't handle non-finite values.
Results may differ from a plain program's by a relative error of at most 0.000073.
Values sent between devices are 32-bit elements; how exact they have to be, the bound alone decides.
A program may use at most 64 MiB of HBM per device.

v0:
```python
import jax
import jax.numpy as jnp
from jax import lax
from jax.sharding import PartitionSpec as P

NPHI = 2048
LMAX = 1024


precise = lax.Precision.HIGHEST


def cut_along(x, dim, count):
    before, after = (x.shape[:dim], x.shape[dim + 1 :])
    return jnp.moveaxis(x.reshape(*before, count, -1, *after), dim, 0)


def summed_on_arrival(x, axis, dim):
    count = lax.axis_size(axis)
    blocks = lax.all_to_all(cut_along(x, dim, count), axis, 0, 0, tiled=True)
    return jnp.sum(blocks, axis=0)


def side_by_side(arrays, axis, dim, along):
    widths = [a.shape[along] for a in arrays]
    both = jnp.concatenate(arrays, axis=along)
    whole = summed_on_arrival(both, axis, dim)
    return tuple(jnp.split(whole, [sum(widths[:k]) for k in range(1, len(widths))], axis=along))


def twiddle_pair(count_rows, count_cols, modulus):
    row_index = jnp.arange(count_rows, dtype=jnp.int32)[:, None]
    col_index = jnp.arange(count_cols, dtype=jnp.int32)[None, :]
    phases = 2.0 * jnp.pi / modulus * (row_index * col_index % modulus).astype(jnp.float32)
    return (jnp.cos(phases), jnp.sin(phases))


def noise_filter(scan_lines, response):
    line_count, length = scan_lines.shape
    log_size = length.bit_length() - 1
    inner_len = 1 << log_size // 2
    outer_len = length // inner_len
    cos_outer, sin_outer = twiddle_pair(outer_len, outer_len, outer_len)
    cos_inner, sin_inner = twiddle_pair(inner_len, inner_len, inner_len)
    twist_cos, twist_sin = twiddle_pair(outer_len, inner_len, length)
    shaped = scan_lines.reshape(line_count, outer_len, inner_len)
    first_real = jnp.einsum("lna,nk->lka", shaped, cos_outer, precision=precise)
    first_imag = -jnp.einsum("lna,nk->lka", shaped, sin_outer, precision=precise)
    turned_real = first_real * twist_cos + first_imag * twist_sin
    turned_imag = first_imag * twist_cos - first_real * twist_sin
    spec_real = jnp.einsum("lka,aj->lkj", turned_real, cos_inner, precision=precise) + jnp.einsum(
        "lka,aj->lkj", turned_imag, sin_inner, precision=precise
    )
    spec_imag = jnp.einsum("lka,aj->lkj", turned_imag, cos_inner, precision=precise) - jnp.einsum(
        "lka,aj->lkj", turned_real, sin_inner, precision=precise
    )
    weights_k = response.reshape(line_count, inner_len, outer_len).transpose(0, 2, 1)
    spec_real = spec_real * weights_k
    spec_imag = spec_imag * weights_k
    back_real = jnp.einsum("lkj,jn->lkn", spec_real, cos_inner, precision=precise) - jnp.einsum(
        "lkj,jn->lkn", spec_imag, sin_inner, precision=precise
    )
    back_imag = jnp.einsum("lkj,jn->lkn", spec_imag, cos_inner, precision=precise) + jnp.einsum(
        "lkj,jn->lkn", spec_real, sin_inner, precision=precise
    )
    untwist_real = back_real * twist_cos - back_imag * twist_sin
    untwist_imag = back_imag * twist_cos + back_real * twist_sin
    result = jnp.einsum("lkn,km->lmn", untwist_real, cos_outer, precision=precise) - jnp.einsum(
        "lkn,km->lmn", untwist_imag, sin_outer, precision=precise
    )
    return (result / length).reshape(line_count, length)


def local(scan_lines, response, cycle_offset, column, order_slot, legendre):
    filtered = noise_filter(scan_lines, response)
    band_cycles = legendre.shape[1]
    flat_index = (cycle_offset * NPHI + column).reshape(-1)
    partial_value = (
        jnp.zeros((band_cycles * NPHI,), jnp.float32)
        .at[flat_index]
        .add(filtered.reshape(-1))
        .reshape(band_cycles, NPHI)
    )
    counts = (
        jnp.zeros((band_cycles * NPHI,), jnp.float32)
        .at[flat_index]
        .add(1.0)
        .reshape(band_cycles, NPHI)
    )
    summed, hit_total = side_by_side((partial_value, counts), "det", 0, 1)
    sky_map = summed / jnp.maximum(hit_total, 1.0)
    pixel_index = jnp.arange(NPHI, dtype=jnp.int32)[:, None]
    phases = 2.0 * jnp.pi / NPHI * (pixel_index * order_slot[None, :] % NPHI).astype(jnp.float32)
    cycle_real = jnp.dot(
        sky_map, jnp.cos(phases), precision=precise, preferred_element_type=jnp.float32
    )
    cycle_imag = -jnp.dot(
        sky_map, jnp.sin(phases), precision=precise, preferred_element_type=jnp.float32
    )
    cycle_modes = jnp.stack([cycle_real, cycle_imag])
    slot_count = legendre.shape[0]
    slot_start = lax.axis_index("det") * slot_count
    local_orders = lax.dynamic_slice_in_dim(order_slot, slot_start, slot_count, 0)
    degree_index = jnp.arange(LMAX, dtype=jnp.int32)
    keep_mask = (degree_index[None, :] >= local_orders[:, None]).astype(jnp.float32)
    terms = (
        jnp.einsum(
            "crs,srl->csl",
            lax.all_to_all(cycle_modes, "det", split_axis=2, concat_axis=1, tiled=True),
            legendre,
            precision=precise,
        )
        * keep_mask[None]
    )
    harmonics = summed_on_arrival(terms, "band", 2)
    return (harmonics, sky_map)


def solution(mesh):
    return jax.shard_map(
        local,
        mesh=mesh,
        in_specs=(
            P(("det", "band"), None),
            P(("det", "band"), None),
            P(("det", "band"), None),
            P(("det", "band"), None),
            P(),
            P("det", "band", None),
        ),
        out_specs=(P(None, "det", "band"), P(("band", "det"), None)),
        check_vma=False,
    )
```

profile of v0, /device:TPU:0, one launch (start us, length us, event | category | flops | bytes accessed | tf_op | source)
XLA Modules:
  0.0 440.6 jit_solution(10654374950417035863)
XLA Ops:
  0.9 1.0 reshape.108
  1.9 0.5 convolution_negate_fusion
  2.5 0.5 fusion.66
  3.1 0.5 fusion.34
  4.4 0.5 fusion.13
  5.4 0.5 fusion.12
  6.4 0.5 convolution_subtract_fusion.1
  7.5 0.5 fusion.39
  8.0 0.5 fusion.11
  9.0 171.3 %scatter_custom_fusion = f32[262144]{0:T(1024)S(1)} fusion(s32[32768]{0:T(1024)S(1)} %bitcast.89, f32[32768]{0:T(1024)S(1)} %reshape.115, f32[]{:T(128)} %constant.55.clone.1), kind=kCustom, calls=%fused_computation.34 | custom fusion | flops 32768 | bytes 1048580 | tf_op jit(solution)/shard_map/scatter-add | solution.py:81
  180.5 171.3 %scatter_custom_fusion.1 = f32[262144]{0:T(1024)S(1)} fusion(s32[32768]{0:T(1024)S(1)} %bitcast.90, f32[32768]{0:T(1024)S(1)} %broadcast.117, f32[]{:T(128)} %constant.55.clone.1), kind=kCustom, calls=%fused_computation.32 | custom fusion | flops 32768 | bytes 1048580 | tf_op jit(solution)/shard_map/scatter-add | solution.py:87
  352.0 1.5 pad_maximum_fusion
  353.5 8.5 %all-to-all-start = ((f32[16,8,4096]{2,1,0:T(8,128)}), f32[16,8,4096]{2,1,0:T(8,128)S(1)}, u32[]{:S(2)}, u32[]{:S(2)}) async-start(f32[16,8,4096]{2,1,0:T(8,128)} %pad_maximum_fusion), calls=%async_computation | async-start | bytes 4194304 | tf_op jit(solution)/shard_map/all_to_all | solution.py:20
  362.0 29.0 %all-to-all-done = f32[16,8,4096]{2,1,0:T(8,128)S(1)} async-done(((f32[16,8,4096]{2,1,0:T(8,128)}), f32[16,8,4096]{2,1,0:T(8,128)S(1)}, u32[]{:S(2)}, u32[]{:S(2)}) %all-to-all-start) | async-done | bytes 2097184 | tf_op jit(solution)/shard_map/all_to_all | solution.py:20
  391.2 8.5 %fusion.15 = f32[1,8,256]{2,1,0:T(8,128)S(1)} fusion(f32[8,2048]{1,0:T(8,128)S(1)} %fusion.47, s32[256]{0:T(256)S(1)} %copy-done.4), kind=kOutput, calls=%fused_computation.28 | convolution fusion | flops 57671680 | bytes 74752 | tf_op jit(solution)/shard_map/dot_general | solution.py:94
  399.7 8.8 %fusion.21 = f32[1,8,256]{2,1,0:T(8,128)S(1)} fusion(f32[8,2048]{1,0:T(8,128)S(1)} %fusion.47, s32[256]{0:T(256)S(1)} %copy-done.4), kind=kOutput, calls=%fused_computation.30 | convolution fusion | flops 57673728 | bytes 74752 | tf_op jit(solution)/shard_map/dot_general | solution.py:97
  408.7 1.0 reshape.141
  409.7 3.5 all-to-all-start.1
  413.3 7.5 %all-to-all-done.1 = f32[16,1,256]{2,1,0:T(1,128)S(1)} async-done(((f32[16,1,256]{2,1,0:T(1,128)}), f32[16,1,256]{2,1,0:T(1,128)S(1)}, u32[]{:S(2)}, u32[]{:S(2)}) %all-to-all-start.1) | async-done | bytes 16416 | tf_op jit(solution)/shard_map/all_to_all | solution.py:109
  420.7 0.5 broadcast.218
  421.2 0.7 reduce
  422.6 6.4 %fusion.14 = f32[16,1,8,2,128]{4,3,2,1,0:T(2,128)S(1)} fusion(f32[2,128,16]{1,0,2:T(2,128)S(1)} %copy.70, f32[16,128,1024]{2,1,0:T(8,128)} %param.11, f32[16,1024]{1,0:T(8,128)S(1)} %fusion.48), kind=kOutput, calls=%fused_computation.27 | convolution fusion | flops 50364416 | bytes 8601600 | tf_op jit(solution)/shard_map/crs,srl->csl/dot_general | solution.py:107
  429.0 10.9 %all_to_all.28 = f32[8,2,16,128]{3,1,2,0:T(2,128)S(1)} all-to-all(f32[8,2,16,128]{3,1,2,0:T(2,128)S(1)} %bitcast.88), channel_id=1, replica_groups=mesh['det'=16,'band'=8] {'band'}, dimensions={0} | all-to-all | bytes 262144 | tf_op jit(solution)/shard_map/all_to_all | solution.py:20
  439.9 0.6 copy.73
  (38 shorter events, 4.6 us)
Async XLA Ops:
  0.6 3.5 copy-start
  6.4 2.2 copy-start.1
  6.4 2.2 copy-start.2
  353.5 8.5 %copy-start.4 = (s32[256]{0:T(256)S(1)}, s32[256]{0:T(256)}, u32[]{:S(2)}) copy-start(s32[256]{0:T(256)} %param.10) | copy-start | bytes 3076
  353.5 37.6 %all-to-all-start = ((f32[16,8,4096]{2,1,0:T(8,128)}), f32[16,8,4096]{2,1,0:T(8,128)S(1)}, u32[]{:S(2)}, u32[]{:S(2)}) async-start(f32[16,8,4096]{2,1,0:T(8,128)} %pad_maximum_fusion), calls=%async_computation | async-start | bytes 4194304 | tf_op jit(solution)/shard_map/all_to_all | solution.py:20
  391.2 8.6 %copy-start.3 = (f32[8,2048]{1,0:T(8,128)}, f32[8,2048]{1,0:T(8,128)S(1)}, u32[]{:S(2)}) copy-start(f32[8,2048]{1,0:T(8,128)S(1)} %fusion.47) | copy-start | bytes 196612
  409.7 11.0 %all-to-all-start.1 = ((f32[16,1,256]{2,1,0:T(1,128)}), f32[16,1,256]{2,1,0:T(1,128)S(1)}, u32[]{:S(2)}, u32[]{:S(2)}) async-start(f32[16,1,256]{2,1,0:T(1,128)} %reshape.141), calls=%async_computation.1 | async-start | bytes 32768 | tf_op jit(solution)/shard_map/all_to_all | solution.py:109
where the time goes:
time: 441 us
  other arithmetic  345 us (78%)
  waiting for transfers between devices  36.4 us (8%)
  matrix products  29.8 us (7%)
  starting transfers between devices  12 us (3%)
  blocking collectives  10.9 us (2%)
  local copies, waits for them, and re-layouts  5.01 us (1%)
    scatter-add x1, other arithmetic, local(): partial_value = jnp.zeros((band_cycles * NPHI,), jnp.float32).at[flat_ind...  171 us
    scatter-add x1, other arithmetic, local(): counts = jnp.zeros((band_cycles * NPHI,), jnp.float32).at[flat_index].add...  171 us
    all_to_all x1, waiting for transfers between devices, summed_on_arrival(): blocks = lax.all_to_all(cut_along(x, dim, count), axis, 0, 0, tiled=True)  29 us
    all_to_all x1, blocking collectives, summed_on_arrival(): blocks = lax.all_to_all(cut_along(x, dim, count), axis, 0, 0, tiled=True)  10.9 us
  transfers between devices with their start and end apart: 2, of which 2 were waited for; matrix products, arithmetic and copies ran while one was open for 0% of the time, Pallas kernels for 0%

commit v1 on v0

--- a/solution.py
+++ b/solution.py
@@ -1,6 +1,10 @@
+import functools
+
 import jax
 import jax.numpy as jnp
 from jax import lax
+from jax.experimental import pallas as pl
+from jax.experimental.pallas import tpu as pltpu
 from jax.sharding import PartitionSpec as P
 
 NPHI = 2048
@@ -71,22 +75,51 @@
     return (result / length).reshape(line_count, length)
 
 
+def one_hot(index, count):
+    own = lax.broadcasted_iota(jnp.int32, (count, index.shape[1]), 0)
+    wide = jnp.broadcast_to(index.astype(jnp.float32), own.shape)
+    return wide.astype(jnp.bfloat16) == own.astype(jnp.float32).astype(jnp.bfloat16)
+
+
+def bin_kernel(cycles, block, value_ref, cycle_ref, column_ref, out_ref):
+    lines, length = value_ref.shape
+    out_ref[...] = jnp.zeros_like(out_ref)
+    steps = length // block
+    zero, one = jnp.bfloat16(0), jnp.bfloat16(1)
+
+    def step(t, carry):
+        line, start = t // steps, pl.multiple_of(t % steps * block, block)
+        where = (pl.ds(line, 1), pl.ds(start, block))
+        value, cycle, column = value_ref[where], cycle_ref[where], column_ref[where]
+        high = value.astype(jnp.bfloat16).astype(jnp.float32)
+        low = value - high
+        hit = one_hot(cycle, cycles)
+        spread = lambda x: jnp.where(hit, jnp.broadcast_to(x, hit.shape).astype(jnp.bfloat16), zero)
+        rows = jnp.concatenate([spread(high), spread(low), jnp.where(hit, one, zero)], 0)
+        cols = jnp.concatenate(
+            [jnp.where(one_hot(column - n, 256), one, zero) for n in range(0, NPHI, 256)], 0
+        )
+        out_ref[...] += lax.dot_general(
+            rows, cols, (((1,), (1,)), ((), ())), preferred_element_type=jnp.float32
+        )
+        return carry
+
+    lax.fori_loop(0, lines * steps, step, 0)
+
+
+def bin_samples(value, cycle, column, cycles):
+    out = pl.pallas_call(
+        functools.partial(bin_kernel, cycles, 1024),
+        out_shape=jax.ShapeDtypeStruct((3 * cycles, NPHI), jnp.float32),
+        compiler_params=pltpu.CompilerParams(vmem_limit_bytes=60 * 2**20),
+    )(value, cycle, column)
+    return out[:cycles] + out[cycles : 2 * cycles], out[2 * cycles :]
+
+
 def local(scan_lines, response, cycle_offset, column, order_slot, legendre):
     filtered = noise_filter(scan_lines, response)
     band_cycles = legendre.shape[1]
-    flat_index = (cycle_offset * NPHI + column).reshape(-1)
-    partial_value = (
-        jnp.zeros((band_cycles * NPHI,), jnp.float32)
-        .at[flat_index]
-        .add(filtered.reshape(-1))
-        .reshape(band_cycles, NPHI)
-    )
-    counts = (
-        jnp.zeros((band_cycles * NPHI,), jnp.float32)
-        .at[flat_index]
-        .add(1.0)
-        .reshape(band_cycles, NPHI)
-    )
+    partial_value, counts = bin_samples(filtered, cycle_offset, column, band_cycles)
     summed, hit_total = side_by_side((partial_value, counts), "det", 0, 1)
     sky_map = summed / jnp.maximum(hit_total, 1.0)
     pixel_index = jnp.arange(NPHI, dtype=jnp.int32)[:, None]

time: 441 us -> 162 us (0.37)
  other arithmetic: 345 us -> 4.76 us
  Pallas kernels: 0 us -> 61.6 us
    scatter-add x2 -> x0, other arithmetic: 343 us -> none  [the longest x1 171 us: local(): partial_value = jnp.zeros((band_cycles * NPHI,), jnp.float32).at[flat_ind...]
    pallas_call x0 -> x1, Pallas kernels: none -> 61.6 us  [bin_samples(): pl.pallas_call(functools.partial(bin_kernel, cycles, 1024), out_shape=jax...]
where the time goes in v1:
time: 162 us
  Pallas kernels  61.6 us (38%)
  waiting for transfers between devices  36.4 us (22%)
  matrix products  29.8 us (18%)
  starting transfers between devices  12 us (7%)
  blocking collectives  10.9 us (7%)
  local copies, waits for them, and re-layouts  5.2 us (3%)
  other arithmetic  4.76 us (3%)
    pallas_call x1, Pallas kernels, bin_samples(): pl.pallas_call(functools.partial(bin_kernel, cycles, 1024), out_shape=jax...  61.6 us
    all_to_all x1, waiting for transfers between devices, summed_on_arrival(): blocks = lax.all_to_all(cut_along(x, dim, count), axis, 0, 0, tiled=True)  29 us
    all_to_all x1, blocking collectives, summed_on_arrival(): blocks = lax.all_to_all(cut_along(x, dim, count), axis, 0, 0, tiled=True)  10.9 us
    dot_general x1, matrix products, local(): jnp.dot(sky_map, jnp.sin(phases), precision=precise, preferred_element_ty...  8.82 us
    dot_general x1, matrix products, local(): jnp.dot(sky_map, jnp.cos(phases), precision=precise, preferred_element_ty...  8.53 us
    all_to_all x1, starting transfers between devices, summed_on_arrival(): blocks = lax.all_to_all(cut_along(x, dim, count), axis, 0, 0, tiled=True)  8.48 us
    all_to_all x1, waiting for transfers between devices, local(): lax.all_to_all(cycle_modes, 'det', split_axis=2, concat_axis=1, tiled=True)  7.45 us
    dot_general x1, matrix products, local(): jnp.einsum('crs,srl->csl', lax.all_to_all(cycle_modes, 'det', split_axis=...  6.36 us
  transfers between devices with their start and end apart: 2, of which 2 were waited for; matrix products, arithmetic and copies ran while one was open for 0% of the time, Pallas kernels for 0%

profile of v1, /device:TPU:0, one launch (start us, length us, event | category | flops | bytes accessed | tf_op | source)
XLA Modules:
  0.0 161.5 jit_solution(3901231471004939345)
XLA Ops:
  0.9 1.0 reshape.75
  1.9 0.5 convolution_negate_fusion
  2.5 0.5 fusion.62
  3.1 0.5 fusion.30
  5.4 0.5 fusion.12
  6.4 0.5 convolution_subtract_fusion.1
  7.4 0.5 fusion.35
  8.0 0.5 fusion.11
  8.5 0.8 reshape.77.value_ref
  9.3 61.6 %shard_map.77 = f32[384,2048]{1,0:T(8,128)} custom-call(f32[8,4096]{1,0:T(8,128)} %reshape.77.value_ref, s32[8,4096]{1,0:T(8,128)} %cycle_ref.1, s32[8,4096]{1,0:T(8,128)} %column_ref.1), custom_call_target="tpu_custom_call" | custom-call | tf_op jit(solution)/shard_map/pallas_call | solution.py:111
  70.9 2.0 %slice_add_fusion = (f32[128,2048]{1,0:T(8,128)S(1)}, f32[128,2048]{1,0:T(8,128)S(1)}) fusion(f32[384,2048]{1,0:T(8,128)} %shard_map.77), kind=kLoop, calls=%fused_computation.29 | loop fusion | flops 262144 | bytes 5242880 | tf_op jit(solution)/shard_map/add | solution.py:116
  72.9 1.5 maximum_bitcast_fusion
  74.4 8.5 %all-to-all-start = ((f32[16,8,4096]{2,1,0:T(8,128)}), f32[16,8,4096]{2,1,0:T(8,128)S(1)}, u32[]{:S(2)}, u32[]{:S(2)}) async-start(f32[16,8,4096]{2,1,0:T(8,128)} %maximum_bitcast_fusion), calls=%async_computation | async-start | bytes 4194304 | tf_op jit(solution)/shard_map/all_to_all | solution.py:24
  83.0 29.0 %all-to-all-done = f32[16,8,4096]{2,1,0:T(8,128)S(1)} async-done(((f32[16,8,4096]{2,1,0:T(8,128)}), f32[16,8,4096]{2,1,0:T(8,128)S(1)}, u32[]{:S(2)}, u32[]{:S(2)}) %all-to-all-start) | async-done | bytes 2097184 | tf_op jit(solution)/shard_map/all_to_all | solution.py:24
  112.1 8.5 %fusion.15 = f32[1,8,256]{2,1,0:T(8,128)S(1)} fusion(f32[8,2048]{1,0:T(8,128)S(1)} %fusion.43, s32[256]{0:T(256)S(1)} %copy-done.2), kind=kOutput, calls=%fused_computation.26 | convolution fusion | flops 57671680 | bytes 74752 | tf_op jit(solution)/shard_map/dot_general | solution.py:127
  120.7 8.8 %fusion.21 = f32[1,8,256]{2,1,0:T(8,128)S(1)} fusion(f32[8,2048]{1,0:T(8,128)S(1)} %fusion.43, s32[256]{0:T(256)S(1)} %copy-done.2), kind=kOutput, calls=%fused_computation.28 | convolution fusion | flops 57673728 | bytes 74752 | tf_op jit(solution)/shard_map/dot_general | solution.py:130
  129.7 1.0 reshape.90
  130.7 3.5 %all-to-all-start.1 = ((f32[16,1,256]{2,1,0:T(1,128)}), f32[16,1,256]{2,1,0:T(1,128)S(1)}, u32[]{:S(2)}, u32[]{:S(2)}) async-start(f32[16,1,256]{2,1,0:T(1,128)} %reshape.90), calls=%async_computation.1 | async-start | bytes 32768 | tf_op jit(solution)/shard_map/all_to_all | solution.py:142
  134.3 7.5 %all-to-all-done.1 = f32[16,1,256]{2,1,0:T(1,128)S(1)} async-done(((f32[16,1,256]{2,1,0:T(1,128)}), f32[16,1,256]{2,1,0:T(1,128)S(1)}, u32[]{:S(2)}, u32[]{:S(2)}) %all-to-all-start.1) | async-done | bytes 16416 | tf_op jit(solution)/shard_map/all_to_all | solution.py:142
  141.7 0.5 broadcast.185
  142.2 0.7 reduce
  143.5 6.4 %fusion.14 = f32[16,1,8,2,128]{4,3,2,1,0:T(2,128)S(1)} fusion(f32[2,128,16]{1,0,2:T(2,128)S(1)} %copy.51, f32[16,128,1024]{2,1,0:T(8,128)} %param.11, f32[16,1024]{1,0:T(8,128)S(1)} %fusion.44), kind=kOutput, calls=%fused_computation.25 | convolution fusion | flops 50364416 | bytes 8601600 | tf_op jit(solution)/shard_map/crs,srl->csl/dot_general | solution.py:140
  150.0 10.9 %all_to_all.28 = f32[8,2,16,128]{3,1,2,0:T(2,128)S(1)} all-to-all(f32[8,2,16,128]{3,1,2,0:T(2,128)S(1)} %bitcast.83), channel_id=1, replica_groups=mesh['det'=16,'band'=8] {'band'}, dimensions={0} | all-to-all | bytes 262144 | tf_op jit(solution)/shard_map/all_to_all | solution.py:24
  160.9 0.6 copy.54
  (28 shorter events, 4.3 us)
Async XLA Ops:
  0.6 3.5 %copy-start = (f32[8,4096]{1,0:T(8,128)S(1)}, f32[8,4096]{1,0:T(8,128)}, u32[]{:S(2)}) copy-start(f32[8,4096]{1,0:T(8,128)} %param.7) | copy-start | bytes 393220
  74.4 8.5 %copy-start.2 = (s32[256]{0:T(256)S(1)}, s32[256]{0:T(256)}, u32[]{:S(2)}) copy-start(s32[256]{0:T(256)} %param.10) | copy-start | bytes 3076
  74.4 37.6 %all-to-all-start = ((f32[16,8,4096]{2,1,0:T(8,128)}), f32[16,8,4096]{2,1,0:T(8,128)S(1)}, u32[]{:S(2)}, u32[]{:S(2)}) async-start(f32[16,8,4096]{2,1,0:T(8,128)} %maximum_bitcast_fusion), calls=%async_computation | async-start | bytes 4194304 | tf_op jit(solution)/shard_map/all_to_all | solution.py:24
  112.1 8.6 %copy-start.1 = (f32[8,2048]{1,0:T(8,128)}, f32[8,2048]{1,0:T(8,128)S(1)}, u32[]{:S(2)}) copy-start(f32[8,2048]{1,0:T(8,128)S(1)} %fusion.43) | copy-start | bytes 196612
  130.7 11.0 %all-to-all-start.1 = ((f32[16,1,256]{2,1,0:T(1,128)}), f32[16,1,256]{2,1,0:T(1,128)S(1)}, u32[]{:S(2)}, u32[]{:S(2)}) async-start(f32[16,1,256]{2,1,0:T(1,128)} %reshape.90), calls=%async_computation.1 | async-start | bytes 32768 | tf_op jit(solution)/shard_map/all_to_all | solution.py:142
